TPU v7x, 128 devices: a whole 4x4x4 slice. The times are simulated.
128 devices in a mesh: section: 4 (over x_lo, core), ctx: 8 (over x_hi, z), tp: 4 (over y).
Axes of the slice: x: 4 (x_hi: 2, x_lo: 2; x = x_hi * 2 + x_lo), y: 4, z: 4, core: 2. Of those that a mesh axis runs over, the one named last changes fastest.
Arguments:
- stretch_order: int32 [8, 2], replicated, may hold values from 0 to 15, as said below
- queries: bfloat16 [4, 4096, 2048], P('section', 'ctx', 'tp'), may hold values from -60 to 60
- key_rows: bfloat16 [4, 4096, 512], P('section', 'ctx', 'tp'), may hold values from -7 to 7
- value_rows: bfloat16 [4, 4096, 512], P('section', 'ctx', 'tp'), may hold values from -5 to 5
- out_grad: bfloat16 [4, 4096, 4096], P('section', ('ctx', 'tp')), may hold values from -6 to 6
- query_weight: bfloat16 [4, 4096, 2048], P('section', None, 'tp'), may hold values from -0.09375 to 0.09375
- key_weight: bfloat16 [4, 4096, 512], P('section', None, 'tp'), may hold values from -0.09375 to 0.09375
- value_weight: bfloat16 [4, 4096, 512], P('section', None, 'tp'), may hold values from -0.09375 to 0.09375
- output_weight: bfloat16 [4, 2048, 4096], P('section', 'tp'), may hold values from -0.125 to 0.125
Outputs:
- sent_grad: bfloat16 [4, 4096, 4096], P('section', ('ctx', 'tp'))
- key_grad: bfloat16 [4, 4096, 512], P('section', 'ctx', 'tp')
- value_grad: bfloat16 [4, 4096, 512], P('section', 'ctx', 'tp')
Inputs may be any that keep to these rules, and one draw needn't show every extreme that they name: `stretch_order`: row c lists the ids of the two blocks of 256 consecutive positions stored, in that order, at ctx index c; the two ids of a row sum to 15 and every id occurs once.
All inputs are finite; a program needn't handle non-finite values.
Results may differ from a plain program's by a relative error of at most 0.015.
Values may be sent and summed in bfloat16 or wider, within the bound.
No kernel may reach another device: no remote copies, remote signals or barrier semaphores. Data moves between devices by JAX's collectives and lax.ppermute only.
A program may use at most 128 MiB of HBM per device.

v0:
```python
import jax
import jax.numpy as jnp
from jax import lax
from jax.sharding import PartitionSpec as P

HD = 128
HQ = 16
KV = 4
NEG_LARGE = -1e30


def shifted(block, axis, distance):
    devices = range(lax.axis_size(axis))
    route = [((i - distance) % len(devices), i) for i in devices]
    return lax.ppermute(block, axis, route)


def contract_last(lhs, rhs):
    return lax.dot_general(lhs, rhs, (((1,), (1,)), ((), ())), preferred_element_type=jnp.float32)


def key_positions(flat_order, offset, row_count, block_len):
    row_ids = offset + jnp.arange(row_count, dtype=jnp.int32)
    owner = row_ids // block_len
    table = jnp.arange(flat_order.shape[0], dtype=jnp.int32)
    picked = jnp.sum(jnp.where(owner[:, None] == table[None, :], flat_order[None, :], 0), axis=1)
    return picked * block_len + row_ids % block_len


def block_scores(query_blk, grad_blk, key_blk, value_blk, score_scale):
    scores = (
        jnp.einsum("qghe,kge->ghqk", query_blk, key_blk, preferred_element_type=jnp.float32)
        * score_scale
    )
    grad_probs = jnp.einsum(
        "qghe,kge->ghqk", grad_blk, value_blk, preferred_element_type=jnp.float32
    )
    return (scores, grad_probs)


def stats_update(running, query_blk, grad_blk, query_pos, key_blk, value_blk, key_pos, score_scale):
    run_max, run_sum, run_dot = running
    scores, grad_probs = block_scores(query_blk, grad_blk, key_blk, value_blk, score_scale)
    visible = key_pos[None, :] <= query_pos[:, None]
    masked = jnp.where(visible, scores, NEG_LARGE)
    new_max = jnp.maximum(run_max, jnp.max(masked, axis=-1))
    weights = jnp.where(visible, jnp.exp(masked - new_max[..., None]), 0.0)
    factor = jnp.exp(run_max - new_max)
    new_sum = run_sum * factor + jnp.sum(weights, axis=-1)
    new_dot = run_dot * factor + jnp.sum(weights * grad_probs, axis=-1)
    return (new_max, new_sum, new_dot)


def block_grads(query_part, key_blk, value_blk, key_pos, score_scale):
    query_blk, grad_blk, query_pos, lse_blk, delta_blk = query_part
    scores, grad_probs = block_scores(query_blk, grad_blk, key_blk, value_blk, score_scale)
    visible = key_pos[None, :] <= query_pos[:, None]
    attn_probs = jnp.where(visible, jnp.exp(scores - lse_blk[..., None]), 0.0)
    dscore = attn_probs * (grad_probs - delta_blk[..., None])
    probs_low = attn_probs.astype(jnp.bfloat16)
    dscore_low = dscore.astype(jnp.bfloat16)
    results = []
    results.append(
        jnp.einsum("ghqk,kge->qghe", dscore_low, key_blk, preferred_element_type=jnp.float32)
        * score_scale
    )
    results.append(
        jnp.einsum("ghqk,qghe->kge", dscore_low, query_blk, preferred_element_type=jnp.float32)
        * score_scale
    )
    results.append(
        jnp.einsum("ghqk,qghe->kge", probs_low, grad_blk, preferred_element_type=jnp.float32)
    )
    return tuple(results)


def guarded(query_part, key_blk, value_blk, key_pos, score_scale, zero_like):

    def guarded_active(operands):
        return block_grads(query_part, operands[0], operands[1], operands[2], score_scale)

    def skipped(operands):
        return zero_like

    return lax.cond(
        jnp.min(key_pos) <= jnp.max(query_part[2]),
        guarded_active,
        skipped,
        (key_blk, value_blk, key_pos),
    )


def per_device(
    stretch_order,
    queries,
    key_rows,
    value_rows,
    out_grad,
    query_weight,
    key_weight,
    value_weight,
    output_weight,
):
    score_scale = HD ** (-0.5)
    group_len = HQ // KV
    query_mat = queries[0]
    key_mat = key_rows[0]
    value_mat = value_rows[0]
    tok_dev = query_mat.shape[0]
    block_len = tok_dev // 2
    kv_dev = key_mat.shape[1] // HD
    block_total = 2 * lax.axis_size("ctx")
    flat_order = stretch_order.reshape(-1)
    own_ids = lax.dynamic_slice_in_dim(flat_order, 2 * lax.axis_index("ctx"), 2, 0)
    out_weight = output_weight[0]
    attn_grad = contract_last(
        lax.all_gather(out_grad[0], "tp", axis=0, tiled=True), out_weight
    ).astype(jnp.bfloat16)
    query_four = query_mat.reshape(tok_dev, kv_dev, group_len, HD)
    grad_four = attn_grad.reshape(tok_dev, kv_dev, group_len, HD)
    local_pos = jnp.arange(block_len, dtype=jnp.int32)
    query_halves = []
    for half_idx in range(2):
        query_halves.append(
            (
                query_four[half_idx * block_len : (half_idx + 1) * block_len],
                grad_four[half_idx * block_len : (half_idx + 1) * block_len],
                own_ids[half_idx] * block_len + local_pos,
            )
        )

    def stats_add(running, key_blk, value_blk, key_pos):
        updated = []
        for half_idx in range(2):
            query_blk, grad_blk, query_pos = query_halves[half_idx]

            def stats_active(state):
                return stats_update(
                    state, query_blk, grad_blk, query_pos, key_blk, value_blk, key_pos, score_scale
                )

            def unchanged(state):
                return state

            updated.append(
                lax.cond(
                    jnp.min(key_pos) <= jnp.max(query_pos),
                    stats_active,
                    unchanged,
                    running[half_idx],
                )
            )
        return tuple(updated)

    stat_shape = (kv_dev, group_len, block_len)
    init_one = (
        jnp.full(stat_shape, NEG_LARGE, jnp.float32),
        jnp.zeros(stat_shape, jnp.float32),
        jnp.zeros(stat_shape, jnp.float32),
    )
    init_stats = (init_one, init_one)
    keys_all, values_all = (
        lax.all_gather(key_mat, "ctx", axis=0, tiled=True),
        lax.all_gather(value_mat, "ctx", axis=0, tiled=True),
    )
    keys_three = keys_all.reshape(-1, kv_dev, HD)
    values_three = values_all.reshape(-1, kv_dev, HD)
    seq_rows = keys_three.shape[0]

    def stats_step(block_idx, running):
        offset = block_idx * block_len
        key_blk = lax.dynamic_slice_in_dim(keys_three, offset, block_len, 0)
        value_blk = lax.dynamic_slice_in_dim(values_three, offset, block_len, 0)
        return stats_add(
            running, key_blk, value_blk, key_positions(flat_order, offset, block_len, block_len)
        )

    running = lax.fori_loop(0, block_total, stats_step, init_stats)
    full_parts = []
    for half_idx in range(2):
        run_max, run_sum, run_dot = running[half_idx]
        lse_blk = run_max + jnp.log(run_sum)
        delta_blk = run_dot / run_sum
        full_parts.append(query_halves[half_idx] + (lse_blk, delta_blk))
    zero_query = jnp.zeros((block_len, kv_dev, group_len, HD), jnp.float32)
    zero_keys = jnp.zeros((block_len, kv_dev, HD), jnp.float32)

    def grad_step(block_idx, state):
        query_sums, key_sums, value_sums = state
        offset = block_idx * block_len
        key_blk = lax.dynamic_slice_in_dim(keys_three, offset, block_len, 0)
        value_blk = lax.dynamic_slice_in_dim(values_three, offset, block_len, 0)
        key_pos = key_positions(flat_order, offset, block_len, block_len)
        key_add = zero_keys
        value_add = zero_keys
        new_query = []
        for half_idx in range(2):
            part_query, part_key, part_value = guarded(
                full_parts[half_idx],
                key_blk,
                value_blk,
                key_pos,
                score_scale,
                (zero_query, zero_keys, zero_keys),
            )
            new_query.append(query_sums[half_idx] + part_query)
            key_add = key_add + part_key
            value_add = value_add + part_value
        key_sums = lax.dynamic_update_slice_in_dim(
            key_sums, lax.dynamic_slice_in_dim(key_sums, offset, block_len, 0) + key_add, offset, 0
        )
        value_sums = lax.dynamic_update_slice_in_dim(
            value_sums,
            lax.dynamic_slice_in_dim(value_sums, offset, block_len, 0) + value_add,
            offset,
            0,
        )
        return (tuple(new_query), key_sums, value_sums)

    zero_full = jnp.zeros((seq_rows, kv_dev, HD), jnp.float32)
    query_sums, key_sums, value_sums = lax.fori_loop(
        0, block_total, grad_step, ((zero_query, zero_query), zero_full, zero_full)
    )
    key_own, value_own = (
        lax.psum_scatter(
            key_sums.astype(jnp.bfloat16), "ctx", scatter_dimension=0, tiled=True
        ).astype(jnp.float32),
        lax.psum_scatter(
            value_sums.astype(jnp.bfloat16), "ctx", scatter_dimension=0, tiled=True
        ).astype(jnp.float32),
    )
    query_grad = (
        jnp.concatenate(query_sums, axis=0)
        .reshape(tok_dev, kv_dev * group_len * HD)
        .astype(jnp.bfloat16)
    )
    key_grad = key_own.reshape(tok_dev, kv_dev * HD).astype(jnp.bfloat16)
    value_grad = value_own.reshape(tok_dev, kv_dev * HD).astype(jnp.bfloat16)
    query_mixer = query_weight[0]
    key_mixer = key_weight[0]
    value_mixer = value_weight[0]
    summed = contract_last(query_grad, query_mixer)
    summed = summed + contract_last(key_grad, key_mixer)
    summed = summed + contract_last(value_grad, value_mixer)
    input_grad = lax.psum_scatter(
        summed.astype(jnp.bfloat16), "tp", scatter_dimension=0, tiled=True
    )
    sent_grad = shifted(input_grad, "section", -1)
    return (sent_grad[None], key_grad[None], value_grad[None])


def solution(mesh):
    placed = (
        P(),
        P("section", "ctx", "tp"),
        P("section", "ctx", "tp"),
        P("section", "ctx", "tp"),
        P("section", ("ctx", "tp"), None),
        P("section", None, "tp"),
        P("section", None, "tp"),
        P("section", None, "tp"),
        P("section", "tp", None),
    )
    return jax.shard_map(
        per_device,
        mesh=mesh,
        in_specs=placed,
        out_specs=(
            P("section", ("ctx", "tp"), None),
            P("section", "ctx", "tp"),
            P("section", "ctx", "tp"),
        ),
        check_vma=False,
    )
```

profile of v0, /device:TPU:1, one launch (start us, length us, event | category | flops | bytes accessed | tf_op | source)
XLA Modules:
  0.0 694.0 jit_solution(15591792125867270716)
XLA Ops:
  15.3 45.6 %all-gather.11.cloned.1.call-done = bf16[1,512,4096]{2,1,0:T(8,128)(2,1)} async-done(((bf16[1,128,4096]{2,1,0:T(8,128)(2,1)}), bf16[1,512,4096]{2,1,0:T(8,128)(2,1)}) %all-gather.11.cloned.1.call-update) | async-done | bytes 4194320 | tf_op jit(solution)/shard_map/all_gather | solution.py:117
  60.9 5.8 fusion.75
  67.2 41.5 %all-gather.7.cloned.1.call-done = bf16[1,4096,128]{2,1,0:T(8,128)(2,1)} async-done(((bf16[1,512,128]{2,1,0:T(8,128)(2,1)}), bf16[1,4096,128]{2,1,0:T(8,128)(2,1)}) %all-gather.7.cloned.1.call-update) | async-done | bytes 1048592 | tf_op jit(solution)/shard_map/all_gather | solution.py:163
  108.6 47.6 %all-gather.9.cloned.1.call-done = bf16[1,4096,128]{2,1,0:T(8,128)(2,1)} async-done(((bf16[1,512,128]{2,1,0:T(8,128)(2,1)}), bf16[1,4096,128]{2,1,0:T(8,128)(2,1)}) %all-gather.9.cloned.1.call-update) | async-done | bytes 1048592 | tf_op jit(solution)/shard_map/all_gather | solution.py:164
  156.3 86.4 %while.50 = (s32[]{:T(128)}, f32[1,4,256]{2,1,0:T(4,128)S(1)}, f32[1,4,256]{2,1,0:T(4,128)S(1)}, f32[1,4,256]{2,1,0:T(4,128)S(1)}, f32[1,4,256]{2,1,0:T(4,128)S(...) while((s32[]{:T(128)}, f32[1,4,256]{2,1,0:T(4,128)S(1)}, ...), condition=%wide.wide.region_15.16_spmd.clone, body=%wide.wide.region_2.15_spmd.clone.sunk | while | flops 273836032 | bytes 8552063 | solution.py:178
  246.9 218.1 %while.51 = (s32[]{:T(128)}, f32[256,1,4,128]{3,0,2,1:T(8,128)}, f32[256,1,4,128]{3,0,2,1:T(8,128)}, f32[4096,1,128]{2,0,1:T(8,128)}, f32[4096,1,128]{2,0,1:T(8,...) while((s32[]{:T(128)}, f32[256,1,4,128]{3,0,2,1:T(8,128)}, ...), condition=%wide.wide.region_23.24_spmd.clone, body=%wide.wide.region_16.0_spmd.clone.sunk | while | flops 675893248 | bytes 18251352 | solution.py:221
  252.4 2.4 conditional.18
  254.9 3.7 conditional.19
  267.1 2.4 conditional.18
  280.7 2.4 conditional.18
  294.2 2.4 conditional.18
  319.0 2.4 conditional.18
  321.4 3.7 conditional.19
  334.9 2.4 conditional.18
  348.4 2.4 conditional.18
  362.0 2.4 conditional.18
  375.6 2.4 conditional.18
  389.1 2.4 conditional.18
  402.7 2.4 conditional.18
  427.4 2.4 conditional.18
  429.9 3.7 conditional.19
  454.6 2.4 conditional.18
  457.0 3.7 conditional.19
  464.9 2.8 convert_element_type.100
  467.8 2.7 convert_element_type.102
  471.0 7.8 %fusion.70 = f32[512,4096]{1,0:T(8,128)} fusion(bf16[1,4096,512]{2,1,0:T(8,128)(2,1)} %param.26, bf16[256,512]{0,1:T(8,128)(2,1)S(1)} %bitcast.275, bf16[256,512]{0,1:T(8,128)(2,1)S(1)} %bitcast.274), kind=kOutput, calls=%fused_computation.125 | convolution fusion | flops 2148532224 | bytes 13107200 | tf_op jit(solution)/shard_map/dot_general | solution.py:19
  478.8 60.4 %reduce-scatter.4.cloned.1.call-done = bf16[512,1,128]{2,0,1:T(8,128)(2,1)} async-done(((bf16[4096,1,128]{2,0,1:T(8,128)(2,1)}), bf16[512,1,128]{2,0,1:T(8,128)(2,1)}) %reduce-scatter.4.cloned.1.call-update) | async-done | bytes 131088 | tf_op jit(solution)/shard_map/reduce_scatter | solution.py:225
  539.2 5.4 fusion.81
  544.6 70.2 %reduce-scatter.6.cloned.1.call-done = bf16[512,1,128]{2,0,1:T(8,128)(2,1)} async-done(((bf16[4096,1,128]{2,0,1:T(8,128)(2,1)}), bf16[512,1,128]{2,0,1:T(8,128)(2,1)}) %reduce-scatter.6.cloned.1.call-update) | async-done | bytes 131088 | tf_op jit(solution)/shard_map/reduce_scatter | solution.py:228
  614.8 9.0 %add_convert_fusion = bf16[512,4096]{1,0:T(8,128)(2,1)} fusion(f32[512,4096]{1,0:T(8,128)} %fusion.70, f32[512,4096]{1,0:T(8,128)} %fusion.81, bf16[1,4096,128]{2,1,0:T(8,128)(2,1)S(1)} %copy-done.3, bf16[512,1,128]{2,0,1:T(8,128)(2,1)} %reduce-scatter.6.cloned.1.call-done), kind=kOutput, calls=%fused_computation.124 | convolution fusion | flops 543162368 | bytes 22151168 | tf_op jit(solution)/shard_map/dot_general | solution.py:19
  623.8 47.8 %reduce-scatter.8.cloned.1.call-done = bf16[128,4096]{1,0:T(8,128)(2,1)} async-done(((bf16[512,4096]{1,0:T(8,128)(2,1)}), bf16[128,4096]{1,0:T(8,128)(2,1)}) %reduce-scatter.8.cloned.1.call-update) | async-done | bytes 1048592 | tf_op jit(solution)/shard_map/reduce_scatter | solution.py:245
  672.4 13.8 %collective-permute-done = bf16[128,4096]{1,0:T(8,128)(2,1)S(1)} collective-permute-done((bf16[128,4096]{1,0:T(8,128)(2,1)}, bf16[128,4096]{1,0:T(8,128)(2,1)S(1)}, u32[]{:S(2)}, u32[]{:S(2)}) %collective-permute-start) | collective-permute-done | bytes 1048608 | tf_op jit(solution)/shard_map/ppermute | solution.py:15
  (640 shorter events, 269.6 us)
Async XLA Ops:
  7.2 532.0 %copy-start = (bf16[1,4096,128]{2,1,0:T(8,128)(2,1)S(1)}, bf16[1,4096,128]{2,1,0:T(8,128)(2,1)}, u32[]{:S(2)}) copy-start(bf16[1,4096,128]{2,1,0:T(8,128)(2,1)} %param.27) | copy-start | bytes 3145732
  7.2 53.8 %all-gather.11.cloned.1.call-start = ((), (), s32[]{:S(2)}) async-start(), calls=%async_computation.8 | async-start | bytes 5242880 | tf_op jit(solution)/shard_map/all_gather | solution.py:117
  7.9 100.7 %all-gather.7.cloned.1.call-start = ((), (), s32[]{:S(2)}) async-start(), calls=%async_computation.6 | async-start | bytes 1179648 | tf_op jit(solution)/shard_map/all_gather | solution.py:163
  8.7 147.6 %all-gather.9.cloned.1.call-start = ((), (), s32[]{:S(2)}) async-start(), calls=%async_computation.7 | async-start | bytes 1179648 | tf_op jit(solution)/shard_map/all_gather | solution.py:164
  9.4 529.8 %reduce-scatter.4.cloned.1.call-start = ((), (), s32[]{:S(2)}) async-start(), calls=%async_computation.3 | async-start | bytes 1179648 | tf_op jit(solution)/shard_map/reduce_scatter | solution.py:225
  10.2 56.6 %copy-start.4 = (s32[8,2]{1,0:T(8,128)}, s32[8,2]{1,0:T(8,128)S(1)}, u32[]{:S(2)}) copy-start(s32[8,2]{1,0:T(8,128)S(1)} %copy.48) | copy-start | bytes 196
  464.9 5.8 copy-start.2
  464.9 5.9 copy-start.1
  467.7 147.1 %reduce-scatter.6.cloned.1.call-start = ((), (), s32[]{:S(2)}) async-start(), calls=%async_computation.4 | async-start | bytes 1179648 | tf_op jit(solution)/shard_map/reduce_scatter | solution.py:228
  470.5 201.2 %reduce-scatter.8.cloned.1.call-start = ((), (), s32[]{:S(2)}) async-start(), calls=%async_computation.5 | async-start | bytes 5242880 | tf_op jit(solution)/shard_map/reduce_scatter | solution.py:245
  478.8 136.0 %copy-start.3 = (bf16[1,4096,128]{2,1,0:T(8,128)(2,1)S(1)}, bf16[1,4096,128]{2,1,0:T(8,128)(2,1)}, u32[]{:S(2)}) copy-start(bf16[1,4096,128]{2,1,0:T(8,128)(2,1)} %param.28) | copy-start | bytes 3145732
  671.7 14.5 %collective-permute-start = (bf16[128,4096]{1,0:T(8,128)(2,1)}, bf16[128,4096]{1,0:T(8,128)(2,1)S(1)}, u32[]{:S(2)}, u32[]{:S(2)}) collective-permute-start(bf16[128,4096]{1,0:T(8,128)(2,1)} %reduce-scatter.8.cloned.1.call-done), channel_id=1, source_target_pairs={{32,0},{64,32},{96,64},{0,96},{33,1},{65,33},{97,65},{1,97},{34,2}... | collective-permute-start | bytes 3145736 | tf_op jit(solution)/shard_map/ppermute | solution.py:15
Sparse Core Ops, SparseCore 0:
  9.6 51.2 all-gather.10
  63.3 45.3 all-gather.6
  111.0 45.1 all-gather.8
  467.8 71.2 reduce-scatter.3
  543.2 71.5 reduce-scatter.5
  624.0 47.6 reduce-scatter.7
where the time goes:
time: 699 us; the launch traced here: 694 us
  waiting for transfers between devices  329 us (47%)
  other arithmetic  114 us (16%)
  loops' own time  84.3 us (12%)
  matrix products  83.8 us (12%)
  local copies, waits for them, and re-layouts  66.5 us (10%)
  between operations  15.5 us (2%)
    reduce_scatter x1, waiting for transfers between devices, per_device(): lax.psum_scatter(value_sums.astype(jnp.bfloat16), 'ctx', scatter_dimensio...  70.2 us
    reduce_scatter x1, waiting for transfers between devices, per_device(): lax.psum_scatter(key_sums.astype(jnp.bfloat16), 'ctx', scatter_dimension=...  60.4 us
    reduce_scatter x1, waiting for transfers between devices, per_device(): lax.psum_scatter(summed.astype(jnp.bfloat16), 'tp', scatter_dimension=0,...  47.8 us
    all_gather x1, waiting for transfers between devices, per_device(): lax.all_gather(value_mat, 'ctx', axis=0, tiled=True)  47.6 us
    all_gather x1, waiting for transfers between devices, per_device(): lax.all_gather(out_grad[0], 'tp', axis=0, tiled=True)  45.6 us
    all_gather x1, waiting for transfers between devices, per_device(): lax.all_gather(key_mat, 'ctx', axis=0, tiled=True)  41.5 us
    another operation x1, loops' own time, per_device(): running = lax.fori_loop(0, block_total, stats_step, init_stats)  41.3 us
    another operation x1, loops' own time, per_device(): lax.fori_loop(0, block_total, grad_step, ((zero_query, zero_query), zero_...  40.8 us
  transfers between devices with their start and end apart: 7, of which 7 were waited for; matrix products, arithmetic and copies ran while one was open for 4% of the time, Pallas kernels for 0%

commit v1 on v0

--- a/solution.py
+++ b/solution.py
@@ -7,6 +7,13 @@
 HQ = 16
 KV = 4
 NEG_LARGE = -1e30
+
+
+def exchange_gather(x, axis, along):
+    devices = lax.axis_size(axis)
+    blocks = jnp.stack([x for _ in range(devices)])
+    blocks = lax.all_to_all(blocks, axis, split_axis=0, concat_axis=0)
+    return jnp.concatenate(blocks, axis=along)
 
 
 def shifted(block, axis, distance):
@@ -161,7 +168,7 @@
     init_stats = (init_one, init_one)
     keys_all, values_all = (
         lax.all_gather(key_mat, "ctx", axis=0, tiled=True),
-        lax.all_gather(value_mat, "ctx", axis=0, tiled=True),
+        exchange_gather(value_mat, "ctx", 0),
     )
     keys_three = keys_all.reshape(-1, kv_dev, HD)
     values_three = values_all.reshape(-1, kv_dev, HD)

time: 699 us -> 657 us (0.940)
  waiting for transfers between devices: 329 us -> 273 us
  starting transfers between devices: 1.15 us -> 9.42 us
    all_gather x1 -> x0, waiting for transfers between devices: 47.6 us -> none  [per_device(): lax.all_gather(value_mat, 'ctx', axis=0, tiled=True)]
    all_to_all x0 -> x1, starting transfers between devices: none -> 8.31 us  [exchange_gather(): blocks = lax.all_to_all(blocks, axis, split_axis=0, concat_axis=0)]
    all_gather x1, waiting for transfers between devices: 45.6 us -> 37.7 us  [per_device(): lax.all_gather(out_grad[0], 'tp', axis=0, tiled=True)]
  transfers between devices with their start and end apart: 7 -> 7, of which waited for: 7 -> 6; matrix products, arithmetic and copies ran while one was open for 4% -> 4% of each run, Pallas kernels for 0% -> 0%
where the time goes in v1:
time: 657 us; the launch traced here: 652 us
  waiting for transfers between devices  273 us (42%)
  other arithmetic  115 us (18%)
  loops' own time  88.9 us (14%)
  matrix products  83.6 us (13%)
  local copies, waits for them, and re-layouts  66.9 us (10%)
  between operations  15.2 us (2%)
  starting transfers between devices  9.42 us (1%)
    reduce_scatter x1, waiting for transfers between devices, per_device(): lax.psum_scatter(value_sums.astype(jnp.bfloat16), 'ctx', scatter_dimensio...  70.2 us
    reduce_scatter x1, waiting for transfers between devices, per_device(): lax.psum_scatter(key_sums.astype(jnp.bfloat16), 'ctx', scatter_dimension=...  60.7 us
    reduce_scatter x1, waiting for transfers between devices, per_device(): lax.psum_scatter(summed.astype(jnp.bfloat16), 'tp', scatter_dimension=0,...  47.8 us
    another operation x1, loops' own time, per_device(): running = lax.fori_loop(0, block_total, stats_step, init_stats)  43.6 us
    another operation x1, loops' own time, per_device(): lax.fori_loop(0, block_total, grad_step, ((zero_query, zero_query), zero_...  43.1 us
    all_gather x1, waiting for transfers between devices, per_device(): lax.all_gather(key_mat, 'ctx', axis=0, tiled=True)  41.4 us
    all_gather x1, waiting for transfers between devices, per_device(): lax.all_gather(out_grad[0], 'tp', axis=0, tiled=True)  37.7 us
    add x16, other arithmetic, grad_step(): new_query.append(query_sums[half_idx] + part_query)  35.9 us
  transfers between devices with their start and end apart: 7, of which 6 were waited for; matrix products, arithmetic and copies ran while one was open for 4% of the time, Pallas kernels for 0%

profile of v1, /device:TPU:1, one launch (start us, length us, event | category | flops | bytes accessed | tf_op | source)
XLA Modules:
  0.0 651.7 jit_solution(1541437944068220375)
XLA Ops:
  10.7 8.3 %all-to-all-start = ((bf16[8,512,128]{2,1,0:T(8,128)(2,1)}), bf16[8,512,128]{2,1,0:T(8,128)(2,1)}, u32[]{:S(2)}, u32[]{:S(2)}) async-start(bf16[8,512,128]{2,1,0:T(8,128)(2,1)} %stack.3), calls=%async_computation | async-start | bytes 2097152 | tf_op jit(solution)/shard_map/all_to_all | solution.py:15
  23.3 37.7 %all-gather.7.cloned.1.call-done = bf16[1,512,4096]{2,1,0:T(8,128)(2,1)} async-done(((bf16[1,128,4096]{2,1,0:T(8,128)(2,1)}), bf16[1,512,4096]{2,1,0:T(8,128)(2,1)}) %all-gather.7.cloned.1.call-update) | async-done | bytes 4194320 | tf_op jit(solution)/shard_map/all_gather | solution.py:124
  61.0 5.8 fusion.75
  67.2 41.4 %all-gather.5.cloned.1.call-done = bf16[1,4096,128]{2,1,0:T(8,128)(2,1)} async-done(((bf16[1,512,128]{2,1,0:T(8,128)(2,1)}), bf16[1,4096,128]{2,1,0:T(8,128)(2,1)}) %all-gather.5.cloned.1.call-update) | async-done | bytes 1048592 | tf_op jit(solution)/shard_map/all_gather | solution.py:170
  108.7 88.7 %while.50 = (s32[]{:T(128)}, f32[1,4,256]{2,1,0:T(4,128)S(1)}, f32[1,4,256]{2,1,0:T(4,128)S(1)}, f32[1,4,256]{2,1,0:T(4,128)S(1)}, f32[1,4,256]{2,1,0:T(4,128)S(...) while((s32[]{:T(128)}, f32[1,4,256]{2,1,0:T(4,128)S(1)}, ...), condition=%wide.wide.region_15.16_spmd.clone, body=%wide.wide.region_2.15_spmd.clone.sunk | while | flops 273836032 | bytes 8552063 | solution.py:185
  201.6 221.0 %while.51 = (s32[]{:T(128)}, f32[256,1,4,128]{3,0,2,1:T(8,128)}, f32[256,1,4,128]{3,0,2,1:T(8,128)}, f32[4096,1,128]{2,0,1:T(8,128)}, f32[4096,1,128]{2,0,1:T(8,...) while((s32[]{:T(128)}, f32[256,1,4,128]{3,0,2,1:T(8,128)}, ...), condition=%wide.wide.region_23.24_spmd.clone, body=%wide.wide.region_16.0_spmd.clone.sunk | while | flops 675893248 | bytes 18251352 | solution.py:228
  207.3 2.4 conditional.18
  209.7 3.8 conditional.19
  222.3 2.4 conditional.18
  236.0 2.4 conditional.18
  249.7 2.4 conditional.18
  274.9 2.4 conditional.18
  277.3 3.8 conditional.19
  291.0 2.4 conditional.18
  304.7 2.4 conditional.18
  318.4 2.4 conditional.18
  332.2 2.4 conditional.18
  345.9 2.4 conditional.18
  359.6 2.4 conditional.18
  384.8 2.4 conditional.18
  387.2 3.8 conditional.19
  412.3 2.4 conditional.18
  414.7 3.8 conditional.19
  422.6 2.8 convert_element_type.100
  425.4 2.7 convert_element_type.102
  428.6 7.8 %fusion.70 = f32[512,4096]{1,0:T(8,128)} fusion(bf16[1,4096,512]{2,1,0:T(8,128)(2,1)} %param.26, bf16[256,512]{0,1:T(8,128)(2,1)S(1)} %bitcast.276, bf16[256,512]{0,1:T(8,128)(2,1)S(1)} %bitcast.275), kind=kOutput, calls=%fused_computation.125 | convolution fusion | flops 2148532224 | bytes 13107200 | tf_op jit(solution)/shard_map/dot_general | solution.py:26
  436.5 60.7 %reduce-scatter.4.cloned.1.call-done = bf16[512,1,128]{2,0,1:T(8,128)(2,1)} async-done(((bf16[4096,1,128]{2,0,1:T(8,128)(2,1)}), bf16[512,1,128]{2,0,1:T(8,128)(2,1)}) %reduce-scatter.4.cloned.1.call-update) | async-done | bytes 131088 | tf_op jit(solution)/shard_map/reduce_scatter | solution.py:232
  497.2 5.4 fusion.81
  502.6 70.2 %reduce-scatter.6.cloned.1.call-done = bf16[512,1,128]{2,0,1:T(8,128)(2,1)} async-done(((bf16[4096,1,128]{2,0,1:T(8,128)(2,1)}), bf16[512,1,128]{2,0,1:T(8,128)(2,1)}) %reduce-scatter.6.cloned.1.call-update) | async-done | bytes 131088 | tf_op jit(solution)/shard_map/reduce_scatter | solution.py:235
  572.8 9.0 %add_convert_fusion = bf16[512,4096]{1,0:T(8,128)(2,1)} fusion(f32[512,4096]{1,0:T(8,128)} %fusion.70, f32[512,4096]{1,0:T(8,128)} %fusion.81, bf16[1,4096,128]{2,1,0:T(8,128)(2,1)S(1)} %copy-done.3, bf16[512,1,128]{2,0,1:T(8,128)(2,1)} %reduce-scatter.6.cloned.1.call-done), kind=kOutput, calls=%fused_computation.124 | convolution fusion | flops 543162368 | bytes 22151168 | tf_op jit(solution)/shard_map/dot_general | solution.py:26
  581.8 47.8 %reduce-scatter.8.cloned.1.call-done = bf16[128,4096]{1,0:T(8,128)(2,1)} async-done(((bf16[512,4096]{1,0:T(8,128)(2,1)}), bf16[128,4096]{1,0:T(8,128)(2,1)}) %reduce-scatter.8.cloned.1.call-update) | async-done | bytes 1048592 | tf_op jit(solution)/shard_map/reduce_scatter | solution.py:252
  630.4 13.8 %collective-permute-done = bf16[128,4096]{1,0:T(8,128)(2,1)S(1)} collective-permute-done((bf16[128,4096]{1,0:T(8,128)(2,1)}, bf16[128,4096]{1,0:T(8,128)(2,1)S(1)}, u32[]{:S(2)}, u32[]{:S(2)}) %collective-permute-start) | collective-permute-done | bytes 1048608 | tf_op jit(solution)/shard_map/ppermute | solution.py:22
  (644 shorter events, 269.9 us)
Async XLA Ops:
  7.2 490.0 %copy-start = (bf16[1,4096,128]{2,1,0:T(8,128)(2,1)S(1)}, bf16[1,4096,128]{2,1,0:T(8,128)(2,1)}, u32[]{:S(2)}) copy-start(bf16[1,4096,128]{2,1,0:T(8,128)(2,1)} %param.27) | copy-start | bytes 3145732
  7.2 11.9 %copy-start.6 = (s32[8,2]{0,1:T(2,128)S(1)}, s32[8,2]{0,1:T(2,128)}, u32[]{:S(2)}) copy-start(s32[8,2]{0,1:T(2,128)} %param.21) | copy-start | bytes 196
  7.2 14.7 %copy-start.4 = (bf16[1,512,512]{2,1,0:T(8,128)(2,1)S(1)}, bf16[1,512,512]{2,1,0:T(8,128)(2,1)}, u32[]{:S(2)}) copy-start(bf16[1,512,512]{2,1,0:T(8,128)(2,1)} %param.22) | copy-start | bytes 1572868
  7.2 53.8 %all-gather.7.cloned.1.call-start = ((), (), s32[]{:S(2)}) async-start(), calls=%async_computation.8 | async-start | bytes 5242880 | tf_op jit(solution)/shard_map/all_gather | solution.py:124
  7.9 100.7 %all-gather.5.cloned.1.call-start = ((), (), s32[]{:S(2)}) async-start(), calls=%async_computation.7 | async-start | bytes 1179648 | tf_op jit(solution)/shard_map/all_gather | solution.py:170
  10.7 56.5 %all-to-all-start = ((bf16[8,512,128]{2,1,0:T(8,128)(2,1)}), bf16[8,512,128]{2,1,0:T(8,128)(2,1)}, u32[]{:S(2)}, u32[]{:S(2)}) async-start(bf16[8,512,128]{2,1,0:T(8,128)(2,1)} %stack.3), calls=%async_computation | async-start | bytes 2097152 | tf_op jit(solution)/shard_map/all_to_all | solution.py:15
  19.0 478.2 %reduce-scatter.4.cloned.1.call-start = ((), (), s32[]{:S(2)}) async-start(), calls=%async_computation.4 | async-start | bytes 1179648 | tf_op jit(solution)/shard_map/reduce_scatter | solution.py:232
  19.1 47.7 %copy-start.5 = (s32[8,2]{1,0:T(8,128)}, s32[8,2]{1,0:T(8,128)S(1)}, u32[]{:S(2)}) copy-start(s32[8,2]{1,0:T(8,128)S(1)} %copy.48) | copy-start | bytes 196
  422.6 5.7 copy-start.2
  422.6 5.9 copy-start.1
  425.4 147.4 %reduce-scatter.6.cloned.1.call-start = ((), (), s32[]{:S(2)}) async-start(), calls=%async_computation.5 | async-start | bytes 1179648 | tf_op jit(solution)/shard_map/reduce_scatter | solution.py:235
  428.1 201.6 %reduce-scatter.8.cloned.1.call-start = ((), (), s32[]{:S(2)}) async-start(), calls=%async_computation.6 | async-start | bytes 5242880 | tf_op jit(solution)/shard_map/reduce_scatter | solution.py:252
  436.5 136.3 %copy-start.3 = (bf16[1,4096,128]{2,1,0:T(8,128)(2,1)S(1)}, bf16[1,4096,128]{2,1,0:T(8,128)(2,1)}, u32[]{:S(2)}) copy-start(bf16[1,4096,128]{2,1,0:T(8,128)(2,1)} %param.28) | copy-start | bytes 3145732
  629.7 14.5 %collective-permute-start = (bf16[128,4096]{1,0:T(8,128)(2,1)}, bf16[128,4096]{1,0:T(8,128)(2,1)S(1)}, u32[]{:S(2)}, u32[]{:S(2)}) collective-permute-start(bf16[128,4096]{1,0:T(8,128)(2,1)} %reduce-scatter.8.cloned.1.call-done), channel_id=1, source_target_pairs={{32,0},{64,32},{96,64},{0,96},{33,1},{65,33},{97,65},{1,97},{34,2}... | collective-permute-start | bytes 3145736 | tf_op jit(solution)/shard_map/ppermute | solution.py:22
Sparse Core Ops, SparseCore 0:
  9.7 51.2 all-gather.6
  63.3 45.2 all-gather.4
  425.5 71.6 reduce-scatter.3
  501.2 71.5 reduce-scatter.5
  582.0 47.6 reduce-scatter.7
